TPU v7x, 768 devices: a whole 4x8x12 slice. The times are simulated.
768 devices in a mesh: mem: 64 (over z_hi, y, core), gx: 4 (over x), gy: 3 (over z_lo).
Axes of the slice: x: 4, y: 8, z: 12 (z_hi: 4, z_lo: 3; z = z_hi * 3 + z_lo), core: 2. Of those that a mesh axis runs over, the one named last changes fastest.
Arguments:
- gradient: float32 [192, 64, 384], P('mem', 'gx', 'gy'), may hold values from -6 to 6
- perturbation: bfloat16 [64, 192, 64, 384], P('mem', None, 'gx', 'gy'), may hold values from -16 to 16
- classes: int32 [2, 64, 384], P(None, 'gx', 'gy'), may hold values from 0 to 3
- land_sea: int32 [64, 384], P('gx', 'gy'), may hold values 0 or 1
Outputs:
- increment: float32 [192, 64, 384], P('mem', 'gx', 'gy')
All inputs are finite; a program needn't handle non-finite values. No bound on the sum of `land_sea` on one device may be relied on, other than what follows from the above.
Results may differ from a plain program's by a relative error of at most 0.0005.
Values sent between devices are 32-bit elements; how exact they have to be, the bound alone decides.
A program may use at most 32 MiB of HBM per device.

v0:
```python
import jax
import jax.numpy as jnp
from jax import lax
from jax.sharding import PartitionSpec as P

LEVELS = 32
STEPS = 8


TABLE = (0.03, 0.07, 0.12, 0.18)


def extended_2(cells, sides, width):
    for axis, dim in sides:
        count = lax.axis_size(axis)
        ends = count - 1
        head = lax.slice_in_dim(cells, 0, width, axis=dim)
        tail = lax.slice_in_dim(cells, cells.shape[dim] - width, cells.shape[dim], axis=dim)
        cells = jnp.concatenate(
            [
                lax.ppermute(tail, axis, [(i, (i + 1) % count) for i in range(ends)]),
                cells,
                lax.ppermute(head, axis, [((i + 1) % count, i) for i in range(ends)]),
            ],
            axis=dim,
        )
    return cells


def lookup(code_map):
    return sum((TABLE[c] * (code_map == c + 1).astype(jnp.float32) for c in range(4)))


def spread(field, coef_x, coef_y, inside):
    centre = field[:, 1:-1, 1:-1]
    centre_in = inside[1:-1, 1:-1]
    east_face = 0.5 * (coef_x[1:-1, 1:-1] + coef_x[2:, 1:-1]) * centre_in * inside[2:, 1:-1]
    west_face = 0.5 * (coef_x[1:-1, 1:-1] + coef_x[:-2, 1:-1]) * centre_in * inside[:-2, 1:-1]
    north_face = 0.5 * (coef_y[1:-1, 1:-1] + coef_y[1:-1, 2:]) * centre_in * inside[1:-1, 2:]
    south_face = 0.5 * (coef_y[1:-1, 1:-1] + coef_y[1:-1, :-2]) * centre_in * inside[1:-1, :-2]
    return (
        centre
        + east_face * (field[:, 2:, 1:-1] - centre)
        + west_face * (field[:, :-2, 1:-1] - centre)
        + north_face * (field[:, 1:-1, 2:] - centre)
        + south_face * (field[:, 1:-1, :-2] - centre)
    )


def per_device(gradient, perturbation, classes, land_sea):
    rim_depth = 1
    members = lax.axis_size("mem")
    width_x = classes.shape[1]
    width_y = classes.shape[2]
    code_map = jnp.stack([classes[0] + 1, classes[1] + 1, land_sea + 1])
    coded = extended_2(code_map, (("gx", 1), ("gy", 2)), rim_depth)
    coef_x = lookup(coded[0])
    coef_y = lookup(coded[1])
    inside = (coded[2] > 0).astype(jnp.float32)
    factor = jnp.where(
        coded[2] == 2,
        jnp.float32(1.0),
        jnp.where(coded[2] == 1, jnp.float32(0.3), jnp.float32(0.0)),
    )

    def crop_to(table, radius):
        offset = rim_depth - radius
        return table[offset : offset + width_x + 2 * radius, offset : offset + width_y + 2 * radius]

    def extend(field):
        return extended_2(field, (("gx", 1), ("gy", 2)), rim_depth)

    def adjoint_group(index, field):
        extended = extend(field)
        extended = spread(
            crop_to(factor, 1) * extended,
            crop_to(coef_x, 1),
            crop_to(coef_y, 1),
            crop_to(inside, 1),
        )
        return extended

    def forward_group(index, field):
        extended = extend(field)
        extended = crop_to(factor, 0) * spread(
            extended, crop_to(coef_x, 1), crop_to(coef_y, 1), crop_to(inside, 1)
        )
        return extended

    all_planes = lax.all_gather(gradient, "mem", axis=0, tiled=True)
    member_block = perturbation[0]
    groups = member_block.shape[0] // LEVELS
    field = jnp.sum(
        (member_block.astype(jnp.float32) * all_planes).reshape(groups, LEVELS, width_x, width_y),
        axis=0,
    )
    field = lax.fori_loop(0, STEPS // rim_depth, adjoint_group, field)
    field = lax.fori_loop(0, STEPS // rim_depth, forward_group, field)
    smoothed = jnp.tile(field, (groups, 1, 1))
    scale = jnp.float32(1.0 / (members - 1))
    terms = member_block.astype(jnp.float32) * smoothed * scale
    increment = lax.psum_scatter(terms, "mem", scatter_dimension=0, tiled=True)
    return increment


def solution(mesh):
    placed = (P("mem", "gx", "gy"), P("mem", None, "gx", "gy"), P(None, "gx", "gy"), P("gx", "gy"))
    return jax.shard_map(
        per_device, mesh=mesh, in_specs=placed, out_specs=P("mem", "gx", "gy"), check_vma=False
    )
```

profile of v0, /device:TPU:1, one launch (start us, length us, event | category | flops | bytes accessed | tf_op | source)
XLA Modules:
  0.0 627.0 jit_solution(13146606781519225073)
XLA Ops:
  8.7 3.9 collective-permute-start.8
  14.0 3.0 collective-permute-done.9
  17.1 4.0 collective-permute-start.10
  22.4 4.0 collective-permute-done.11
  26.7 84.2 %all-gather.2.cloned.1.call-done = f32[192,16,128]{2,1,0:T(8,128)} async-done(((f32[3,16,128]{2,1,0:T(8,128)}), f32[192,16,128]{2,1,0:T(8,128)}) %all-gather.2.cloned.1.call-update) | async-done | bytes 1572880 | tf_op jit(solution)/shard_map/all_gather | solution.py:90
  110.9 1.8 convert_multiply_fusion.1
  112.8 147.4 %while.24 = (s32[]{:T(128)}, f32[32,16,128]{2,1,0:T(8,128)S(1)}, f32[18,130]{1,0:T(8,128)S(1)}, f32[16,128]{1,0:T(8,128)S(1)}, f32[18,130]{1,0:T(8,128)S(1)}, /*...) while((s32[]{:T(128)}, f32[32,16,128]{2,1,0:T(8,128)S(1)}, ...), condition=%wide.region_2.3_spmd, body=%wide.region_1.2_spmd.sunk | while | flops 1332866 | bytes 3134861 | solution.py:97
  114.1 4.0 collective-permute-start.1
  120.5 4.0 collective-permute-start.3
  124.6 5.7 collective-permute-done.2
  133.5 4.0 collective-permute-start.1
  139.8 4.8 collective-permute-start.3
  144.7 3.8 collective-permute-done.2
  151.5 4.3 collective-permute-start.1
  158.2 4.8 collective-permute-start.3
  163.0 3.1 collective-permute-done.2
  169.8 4.3 collective-permute-start.1
  176.5 4.5 collective-permute-start.3
  181.0 3.1 collective-permute-done.2
  187.8 4.3 collective-permute-start.1
  194.5 4.5 collective-permute-start.3
  199.1 3.1 collective-permute-done.2
  205.9 4.5 collective-permute-start.1
  212.8 4.5 collective-permute-start.3
  217.4 3.1 collective-permute-done.2
  224.2 4.5 collective-permute-start.1
  231.1 4.5 collective-permute-start.3
  235.7 3.1 collective-permute-done.2
  242.5 4.5 collective-permute-start.1
  249.5 4.5 collective-permute-start.3
  254.0 3.5 collective-permute-done.2
  257.5 1.8 collective-permute-done.3
  260.2 148.9 %while.25 = (s32[]{:T(128)}, f32[32,16,128]{2,1,0:T(8,128)S(1)}, f32[18,130]{1,0:T(8,128)S(1)}, f32[16,128]{1,0:T(8,128)S(1)}, f32[18,130]{1,0:T(8,128)S(1)}, /*...) while((s32[]{:T(128)}, f32[32,16,128]{2,1,0:T(8,128)S(1)}, ...), condition=%wide.region_4.5_spmd, body=%wide.region_3.4_spmd.sunk | while | flops 1548290 | bytes 2064125 | solution.py:98
  261.7 4.5 collective-permute-start.5
  267.3 3.8 collective-permute-start.6
  272.6 6.9 %collective-permute-done.6 = f32[32,18,1]{2,1,0:T(8,128)S(1)} collective-permute-done((f32[32,18,1]{2,1,0:T(8,128)S(1)}, f32[32,18,1]{2,1,0:T(8,128)S(1)}, u32[]{:S(2)}, u32[]{:S(2)}) %collective-permute-start.6) | collective-permute-done | bytes 2336 | tf_op jit(solution)/shard_map/while/body/eval_jaxpr/ppermute | solution.py:21
  281.7 4.3 collective-permute-start.5
  287.1 3.7 collective-permute-start.6
  292.2 4.6 collective-permute-done.6
  296.8 4.0 collective-permute-done.7
  302.5 4.4 collective-permute-start.5
  308.1 2.6 collective-permute-start.6
  312.2 3.2 collective-permute-done.6
  315.4 3.8 collective-permute-done.7
  321.1 4.3 collective-permute-start.5
  326.4 2.2 collective-permute-start.6
  330.1 3.2 collective-permute-done.6
  333.3 3.8 collective-permute-done.7
  338.9 4.3 collective-permute-start.5
  344.3 1.9 collective-permute-start.6
  347.7 3.2 collective-permute-done.6
  350.9 3.8 collective-permute-done.7
  356.5 4.5 collective-permute-start.5
  362.2 1.9 collective-permute-start.6
  365.6 3.2 collective-permute-done.6
  368.8 3.8 collective-permute-done.7
  374.4 4.8 collective-permute-start.5
  380.3 1.8 collective-permute-start.6
  383.6 3.2 collective-permute-done.6
  386.8 3.8 collective-permute-done.7
  392.4 4.8 collective-permute-start.5
  401.5 3.2 collective-permute-done.6
  404.7 3.9 collective-permute-done.7
  410.5 209.7 %reduce-scatter.2.cloned.1.call-done = f32[3,16,128]{2,1,0:T(8,128)} async-done(((f32[192,16,128]{2,1,0:T(8,128)}), f32[3,16,128]{2,1,0:T(8,128)}) %reduce-scatter.2.cloned.1.call-update) | async-done | bytes 24592 | tf_op jit(solution)/shard_map/reduce_scatter | solution.py:102
  (198 shorter events, 89.0 us)
Async XLA Ops:
  6.5 104.3 %all-gather.2.cloned.1.call-start = ((), (), s32[]{:S(2)}) async-start(), calls=%async_computation.1 | async-start | bytes 1597440 | tf_op jit(solution)/shard_map/all_gather | solution.py:90
  7.3 612.9 %reduce-scatter.2.cloned.1.call-start = ((), (), s32[]{:S(2)}) async-start(), calls=%async_computation.2 | async-start | bytes 1597440 | tf_op jit(solution)/shard_map/reduce_scatter | solution.py:102
  8.7 5.2 collective-permute-start.8
  17.1 5.3 collective-permute-start.10
  21.1 5.3 collective-permute-start.11
  112.8 5.3 collective-permute-start
  119.2 11.1 %collective-permute-start.2 = (f32[32,18,1]{2,1,0:T(8,128)S(1)}, f32[32,18,1]{2,1,0:T(8,128)S(1)}, u32[]{:S(2)}, u32[]{:S(2)}) collective-permute-start(f32[32,18,1]{2,1,0:T(8,128)S(1)} %get-tuple-element.346), channel_id=1, source_target_pairs={{1,0},{2,1},{4,3},{5,4},{7,6},{8,7},{10,9},{11,10},{13,12},{14,13}... | collective-permute-start | bytes 6920 | tf_op jit(solution)/shard_map/while/body/eval_jaxpr/ppermute | solution.py:23
  120.5 10.7 %collective-permute-start.3 = (f32[32,18,1]{2,1,0:T(8,128)S(1)}, f32[32,18,1]{2,1,0:T(8,128)S(1)}, u32[]{:S(2)}, u32[]{:S(2)}) collective-permute-start(f32[32,18,1]{2,1,0:T(8,128)S(1)} %get-tuple-element.347), channel_id=1, source_target_pairs={{0,1},{1,2},{3,4},{4,5},{6,7},{7,8},{9,10},{10,11},{12,13},{13,14}... | collective-permute-start | bytes 6920 | tf_op jit(solution)/shard_map/while/body/eval_jaxpr/ppermute | solution.py:21
  132.2 5.3 collective-permute-start
  138.5 9.9 %collective-permute-start.2 = (f32[32,18,1]{2,1,0:T(8,128)S(1)}, f32[32,18,1]{2,1,0:T(8,128)S(1)}, u32[]{:S(2)}, u32[]{:S(2)}) collective-permute-start(f32[32,18,1]{2,1,0:T(8,128)S(1)} %get-tuple-element.346), channel_id=1, source_target_pairs={{1,0},{2,1},{4,3},{5,4},{7,6},{8,7},{10,9},{11,10},{13,12},{14,13}... | collective-permute-start | bytes 6920 | tf_op jit(solution)/shard_map/while/body/eval_jaxpr/ppermute | solution.py:23
  139.8 9.4 %collective-permute-start.3 = (f32[32,18,1]{2,1,0:T(8,128)S(1)}, f32[32,18,1]{2,1,0:T(8,128)S(1)}, u32[]{:S(2)}, u32[]{:S(2)}) collective-permute-start(f32[32,18,1]{2,1,0:T(8,128)S(1)} %get-tuple-element.347), channel_id=1, source_target_pairs={{0,1},{1,2},{3,4},{4,5},{6,7},{7,8},{9,10},{10,11},{12,13},{13,14}... | collective-permute-start | bytes 6920 | tf_op jit(solution)/shard_map/while/body/eval_jaxpr/ppermute | solution.py:21
  150.2 5.6 collective-permute-start
  151.5 5.1 collective-permute-start.1
  156.9 9.3 %collective-permute-start.2 = (f32[32,18,1]{2,1,0:T(8,128)S(1)}, f32[32,18,1]{2,1,0:T(8,128)S(1)}, u32[]{:S(2)}, u32[]{:S(2)}) collective-permute-start(f32[32,18,1]{2,1,0:T(8,128)S(1)} %get-tuple-element.346), channel_id=1, source_target_pairs={{1,0},{2,1},{4,3},{5,4},{7,6},{8,7},{10,9},{11,10},{13,12},{14,13}... | collective-permute-start | bytes 6920 | tf_op jit(solution)/shard_map/while/body/eval_jaxpr/ppermute | solution.py:23
  158.2 9.4 %collective-permute-start.3 = (f32[32,18,1]{2,1,0:T(8,128)S(1)}, f32[32,18,1]{2,1,0:T(8,128)S(1)}, u32[]{:S(2)}, u32[]{:S(2)}) collective-permute-start(f32[32,18,1]{2,1,0:T(8,128)S(1)} %get-tuple-element.347), channel_id=1, source_target_pairs={{0,1},{1,2},{3,4},{4,5},{6,7},{7,8},{9,10},{10,11},{12,13},{13,14}... | collective-permute-start | bytes 6920 | tf_op jit(solution)/shard_map/while/body/eval_jaxpr/ppermute | solution.py:21
  168.5 5.6 collective-permute-start
  169.8 5.1 collective-permute-start.1
  175.2 9.0 %collective-permute-start.2 = (f32[32,18,1]{2,1,0:T(8,128)S(1)}, f32[32,18,1]{2,1,0:T(8,128)S(1)}, u32[]{:S(2)}, u32[]{:S(2)}) collective-permute-start(f32[32,18,1]{2,1,0:T(8,128)S(1)} %get-tuple-element.346), channel_id=1, source_target_pairs={{1,0},{2,1},{4,3},{5,4},{7,6},{8,7},{10,9},{11,10},{13,12},{14,13}... | collective-permute-start | bytes 6920 | tf_op jit(solution)/shard_map/while/body/eval_jaxpr/ppermute | solution.py:23
  176.5 9.2 %collective-permute-start.3 = (f32[32,18,1]{2,1,0:T(8,128)S(1)}, f32[32,18,1]{2,1,0:T(8,128)S(1)}, u32[]{:S(2)}, u32[]{:S(2)}) collective-permute-start(f32[32,18,1]{2,1,0:T(8,128)S(1)} %get-tuple-element.347), channel_id=1, source_target_pairs={{0,1},{1,2},{3,4},{4,5},{6,7},{7,8},{9,10},{10,11},{12,13},{13,14}... | collective-permute-start | bytes 6920 | tf_op jit(solution)/shard_map/while/body/eval_jaxpr/ppermute | solution.py:21
  186.5 5.6 collective-permute-start
  193.2 9.0 %collective-permute-start.2 = (f32[32,18,1]{2,1,0:T(8,128)S(1)}, f32[32,18,1]{2,1,0:T(8,128)S(1)}, u32[]{:S(2)}, u32[]{:S(2)}) collective-permute-start(f32[32,18,1]{2,1,0:T(8,128)S(1)} %get-tuple-element.346), channel_id=1, source_target_pairs={{1,0},{2,1},{4,3},{5,4},{7,6},{8,7},{10,9},{11,10},{13,12},{14,13}... | collective-permute-start | bytes 6920 | tf_op jit(solution)/shard_map/while/body/eval_jaxpr/ppermute | solution.py:23
  194.5 9.2 %collective-permute-start.3 = (f32[32,18,1]{2,1,0:T(8,128)S(1)}, f32[32,18,1]{2,1,0:T(8,128)S(1)}, u32[]{:S(2)}, u32[]{:S(2)}) collective-permute-start(f32[32,18,1]{2,1,0:T(8,128)S(1)} %get-tuple-element.347), channel_id=1, source_target_pairs={{0,1},{1,2},{3,4},{4,5},{6,7},{7,8},{9,10},{10,11},{12,13},{13,14}... | collective-permute-start | bytes 6920 | tf_op jit(solution)/shard_map/while/body/eval_jaxpr/ppermute | solution.py:21
  204.6 5.9 collective-permute-start
  205.9 5.4 collective-permute-start.1
  211.5 9.0 %collective-permute-start.2 = (f32[32,18,1]{2,1,0:T(8,128)S(1)}, f32[32,18,1]{2,1,0:T(8,128)S(1)}, u32[]{:S(2)}, u32[]{:S(2)}) collective-permute-start(f32[32,18,1]{2,1,0:T(8,128)S(1)} %get-tuple-element.346), channel_id=1, source_target_pairs={{1,0},{2,1},{4,3},{5,4},{7,6},{8,7},{10,9},{11,10},{13,12},{14,13}... | collective-permute-start | bytes 6920 | tf_op jit(solution)/shard_map/while/body/eval_jaxpr/ppermute | solution.py:23
  212.8 9.2 %collective-permute-start.3 = (f32[32,18,1]{2,1,0:T(8,128)S(1)}, f32[32,18,1]{2,1,0:T(8,128)S(1)}, u32[]{:S(2)}, u32[]{:S(2)}) collective-permute-start(f32[32,18,1]{2,1,0:T(8,128)S(1)} %get-tuple-element.347), channel_id=1, source_target_pairs={{0,1},{1,2},{3,4},{4,5},{6,7},{7,8},{9,10},{10,11},{12,13},{13,14}... | collective-permute-start | bytes 6920 | tf_op jit(solution)/shard_map/while/body/eval_jaxpr/ppermute | solution.py:21
  222.9 5.9 collective-permute-start
  224.2 5.4 collective-permute-start.1
  229.8 9.0 %collective-permute-start.2 = (f32[32,18,1]{2,1,0:T(8,128)S(1)}, f32[32,18,1]{2,1,0:T(8,128)S(1)}, u32[]{:S(2)}, u32[]{:S(2)}) collective-permute-start(f32[32,18,1]{2,1,0:T(8,128)S(1)} %get-tuple-element.346), channel_id=1, source_target_pairs={{1,0},{2,1},{4,3},{5,4},{7,6},{8,7},{10,9},{11,10},{13,12},{14,13}... | collective-permute-start | bytes 6920 | tf_op jit(solution)/shard_map/while/body/eval_jaxpr/ppermute | solution.py:23
  231.1 9.2 %collective-permute-start.3 = (f32[32,18,1]{2,1,0:T(8,128)S(1)}, f32[32,18,1]{2,1,0:T(8,128)S(1)}, u32[]{:S(2)}, u32[]{:S(2)}) collective-permute-start(f32[32,18,1]{2,1,0:T(8,128)S(1)} %get-tuple-element.347), channel_id=1, source_target_pairs={{0,1},{1,2},{3,4},{4,5},{6,7},{7,8},{9,10},{10,11},{12,13},{13,14}... | collective-permute-start | bytes 6920 | tf_op jit(solution)/shard_map/while/body/eval_jaxpr/ppermute | solution.py:21
  241.2 5.9 collective-permute-start
  242.5 5.4 collective-permute-start.1
  248.2 9.4 %collective-permute-start.2 = (f32[32,18,1]{2,1,0:T(8,128)S(1)}, f32[32,18,1]{2,1,0:T(8,128)S(1)}, u32[]{:S(2)}, u32[]{:S(2)}) collective-permute-start(f32[32,18,1]{2,1,0:T(8,128)S(1)} %get-tuple-element.346), channel_id=1, source_target_pairs={{1,0},{2,1},{4,3},{5,4},{7,6},{8,7},{10,9},{11,10},{13,12},{14,13}... | collective-permute-start | bytes 6920 | tf_op jit(solution)/shard_map/while/body/eval_jaxpr/ppermute | solution.py:23
  249.5 9.8 %collective-permute-start.3 = (f32[32,18,1]{2,1,0:T(8,128)S(1)}, f32[32,18,1]{2,1,0:T(8,128)S(1)}, u32[]{:S(2)}, u32[]{:S(2)}) collective-permute-start(f32[32,18,1]{2,1,0:T(8,128)S(1)} %get-tuple-element.347), channel_id=1, source_target_pairs={{0,1},{1,2},{3,4},{4,5},{6,7},{7,8},{9,10},{10,11},{12,13},{13,14}... | collective-permute-start | bytes 6920 | tf_op jit(solution)/shard_map/while/body/eval_jaxpr/ppermute | solution.py:21
  260.2 6.0 collective-permute-start.4
  261.7 5.4 collective-permute-start.5
  267.3 12.2 %collective-permute-start.6 = (f32[32,18,1]{2,1,0:T(8,128)S(1)}, f32[32,18,1]{2,1,0:T(8,128)S(1)}, u32[]{:S(2)}, u32[]{:S(2)}) collective-permute-start(f32[32,18,1]{2,1,0:T(8,128)S(1)} %get-tuple-element.362), channel_id=1, source_target_pairs={{0,1},{1,2},{3,4},{4,5},{6,7},{7,8},{9,10},{10,11},{12,13},{13,14}... | collective-permute-start | bytes 6920 | tf_op jit(solution)/shard_map/while/body/eval_jaxpr/ppermute | solution.py:21
  271.2 8.8 %collective-permute-start.7 = (f32[32,18,1]{2,1,0:T(8,128)S(1)}, f32[32,18,1]{2,1,0:T(8,128)S(1)}, u32[]{:S(2)}, u32[]{:S(2)}) collective-permute-start(f32[32,18,1]{2,1,0:T(8,128)S(1)} %get-tuple-element.363), channel_id=1, source_target_pairs={{1,0},{2,1},{4,3},{5,4},{7,6},{8,7},{10,9},{11,10},{13,12},{14,13}... | collective-permute-start | bytes 6920 | tf_op jit(solution)/shard_map/while/body/eval_jaxpr/ppermute | solution.py:23
  280.4 5.6 collective-permute-start.4
  281.7 5.1 collective-permute-start.5
  287.1 9.7 %collective-permute-start.6 = (f32[32,18,1]{2,1,0:T(8,128)S(1)}, f32[32,18,1]{2,1,0:T(8,128)S(1)}, u32[]{:S(2)}, u32[]{:S(2)}) collective-permute-start(f32[32,18,1]{2,1,0:T(8,128)S(1)} %get-tuple-element.362), channel_id=1, source_target_pairs={{0,1},{1,2},{3,4},{4,5},{6,7},{7,8},{9,10},{10,11},{12,13},{13,14}... | collective-permute-start | bytes 6920 | tf_op jit(solution)/shard_map/while/body/eval_jaxpr/ppermute | solution.py:21
  290.8 10.0 %collective-permute-start.7 = (f32[32,18,1]{2,1,0:T(8,128)S(1)}, f32[32,18,1]{2,1,0:T(8,128)S(1)}, u32[]{:S(2)}, u32[]{:S(2)}) collective-permute-start(f32[32,18,1]{2,1,0:T(8,128)S(1)} %get-tuple-element.363), channel_id=1, source_target_pairs={{1,0},{2,1},{4,3},{5,4},{7,6},{8,7},{10,9},{11,10},{13,12},{14,13}... | collective-permute-start | bytes 6920 | tf_op jit(solution)/shard_map/while/body/eval_jaxpr/ppermute | solution.py:23
  301.2 5.8 collective-permute-start.4
  302.5 5.3 collective-permute-start.5
  308.1 7.3 %collective-permute-start.6 = (f32[32,18,1]{2,1,0:T(8,128)S(1)}, f32[32,18,1]{2,1,0:T(8,128)S(1)}, u32[]{:S(2)}, u32[]{:S(2)}) collective-permute-start(f32[32,18,1]{2,1,0:T(8,128)S(1)} %get-tuple-element.362), channel_id=1, source_target_pairs={{0,1},{1,2},{3,4},{4,5},{6,7},{7,8},{9,10},{10,11},{12,13},{13,14}... | collective-permute-start | bytes 6920 | tf_op jit(solution)/shard_map/while/body/eval_jaxpr/ppermute | solution.py:21
  310.8 8.5 %collective-permute-start.7 = (f32[32,18,1]{2,1,0:T(8,128)S(1)}, f32[32,18,1]{2,1,0:T(8,128)S(1)}, u32[]{:S(2)}, u32[]{:S(2)}) collective-permute-start(f32[32,18,1]{2,1,0:T(8,128)S(1)} %get-tuple-element.363), channel_id=1, source_target_pairs={{1,0},{2,1},{4,3},{5,4},{7,6},{8,7},{10,9},{11,10},{13,12},{14,13}... | collective-permute-start | bytes 6920 | tf_op jit(solution)/shard_map/while/body/eval_jaxpr/ppermute | solution.py:23
  319.8 5.6 collective-permute-start.4
  326.4 6.9 %collective-permute-start.6 = (f32[32,18,1]{2,1,0:T(8,128)S(1)}, f32[32,18,1]{2,1,0:T(8,128)S(1)}, u32[]{:S(2)}, u32[]{:S(2)}) collective-permute-start(f32[32,18,1]{2,1,0:T(8,128)S(1)} %get-tuple-element.362), channel_id=1, source_target_pairs={{0,1},{1,2},{3,4},{4,5},{6,7},{7,8},{9,10},{10,11},{12,13},{13,14}... | collective-permute-start | bytes 6920 | tf_op jit(solution)/shard_map/while/body/eval_jaxpr/ppermute | solution.py:21
  328.6 8.5 %collective-permute-start.7 = (f32[32,18,1]{2,1,0:T(8,128)S(1)}, f32[32,18,1]{2,1,0:T(8,128)S(1)}, u32[]{:S(2)}, u32[]{:S(2)}) collective-permute-start(f32[32,18,1]{2,1,0:T(8,128)S(1)} %get-tuple-element.363), channel_id=1, source_target_pairs={{1,0},{2,1},{4,3},{5,4},{7,6},{8,7},{10,9},{11,10},{13,12},{14,13}... | collective-permute-start | bytes 6920 | tf_op jit(solution)/shard_map/while/body/eval_jaxpr/ppermute | solution.py:23
  337.6 5.6 collective-permute-start.4
  344.3 6.6 %collective-permute-start.6 = (f32[32,18,1]{2,1,0:T(8,128)S(1)}, f32[32,18,1]{2,1,0:T(8,128)S(1)}, u32[]{:S(2)}, u32[]{:S(2)}) collective-permute-start(f32[32,18,1]{2,1,0:T(8,128)S(1)} %get-tuple-element.362), channel_id=1, source_target_pairs={{0,1},{1,2},{3,4},{4,5},{6,7},{7,8},{9,10},{10,11},{12,13},{13,14}... | collective-permute-start | bytes 6920 | tf_op jit(solution)/shard_map/while/body/eval_jaxpr/ppermute | solution.py:21
  346.2 8.5 %collective-permute-start.7 = (f32[32,18,1]{2,1,0:T(8,128)S(1)}, f32[32,18,1]{2,1,0:T(8,128)S(1)}, u32[]{:S(2)}, u32[]{:S(2)}) collective-permute-start(f32[32,18,1]{2,1,0:T(8,128)S(1)} %get-tuple-element.363), channel_id=1, source_target_pairs={{1,0},{2,1},{4,3},{5,4},{7,6},{8,7},{10,9},{11,10},{13,12},{14,13}... | collective-permute-start | bytes 6920 | tf_op jit(solution)/shard_map/while/body/eval_jaxpr/ppermute | solution.py:23
  355.2 5.9 collective-permute-start.4
  356.5 5.4 collective-permute-start.5
  362.2 6.6 %collective-permute-start.6 = (f32[32,18,1]{2,1,0:T(8,128)S(1)}, f32[32,18,1]{2,1,0:T(8,128)S(1)}, u32[]{:S(2)}, u32[]{:S(2)}) collective-permute-start(f32[32,18,1]{2,1,0:T(8,128)S(1)} %get-tuple-element.362), channel_id=1, source_target_pairs={{0,1},{1,2},{3,4},{4,5},{6,7},{7,8},{9,10},{10,11},{12,13},{13,14}... | collective-permute-start | bytes 6920 | tf_op jit(solution)/shard_map/while/body/eval_jaxpr/ppermute | solution.py:21
  364.1 8.5 %collective-permute-start.7 = (f32[32,18,1]{2,1,0:T(8,128)S(1)}, f32[32,18,1]{2,1,0:T(8,128)S(1)}, u32[]{:S(2)}, u32[]{:S(2)}) collective-permute-start(f32[32,18,1]{2,1,0:T(8,128)S(1)} %get-tuple-element.363), channel_id=1, source_target_pairs={{1,0},{2,1},{4,3},{5,4},{7,6},{8,7},{10,9},{11,10},{13,12},{14,13}... | collective-permute-start | bytes 6920 | tf_op jit(solution)/shard_map/while/body/eval_jaxpr/ppermute | solution.py:23
  373.1 6.2 collective-permute-start.4
  374.4 5.7 collective-permute-start.5
  380.3 6.4 %collective-permute-start.6 = (f32[32,18,1]{2,1,0:T(8,128)S(1)}, f32[32,18,1]{2,1,0:T(8,128)S(1)}, u32[]{:S(2)}, u32[]{:S(2)}) collective-permute-start(f32[32,18,1]{2,1,0:T(8,128)S(1)} %get-tuple-element.362), channel_id=1, source_target_pairs={{0,1},{1,2},{3,4},{4,5},{6,7},{7,8},{9,10},{10,11},{12,13},{13,14}... | collective-permute-start | bytes 6920 | tf_op jit(solution)/shard_map/while/body/eval_jaxpr/ppermute | solution.py:21
  382.1 8.5 %collective-permute-start.7 = (f32[32,18,1]{2,1,0:T(8,128)S(1)}, f32[32,18,1]{2,1,0:T(8,128)S(1)}, u32[]{:S(2)}, u32[]{:S(2)}) collective-permute-start(f32[32,18,1]{2,1,0:T(8,128)S(1)} %get-tuple-element.363), channel_id=1, source_target_pairs={{1,0},{2,1},{4,3},{5,4},{7,6},{8,7},{10,9},{11,10},{13,12},{14,13}... | collective-permute-start | bytes 6920 | tf_op jit(solution)/shard_map/while/body/eval_jaxpr/ppermute | solution.py:23
  391.1 6.2 collective-permute-start.4
  392.4 5.7 collective-permute-start.5
  398.4 6.4 %collective-permute-start.6 = (f32[32,18,1]{2,1,0:T(8,128)S(1)}, f32[32,18,1]{2,1,0:T(8,128)S(1)}, u32[]{:S(2)}, u32[]{:S(2)}) collective-permute-start(f32[32,18,1]{2,1,0:T(8,128)S(1)} %get-tuple-element.362), channel_id=1, source_target_pairs={{0,1},{1,2},{3,4},{4,5},{6,7},{7,8},{9,10},{10,11},{12,13},{13,14}... | collective-permute-start | bytes 6920 | tf_op jit(solution)/shard_map/while/body/eval_jaxpr/ppermute | solution.py:21
  400.1 8.6 %collective-permute-start.7 = (f32[32,18,1]{2,1,0:T(8,128)S(1)}, f32[32,18,1]{2,1,0:T(8,128)S(1)}, u32[]{:S(2)}, u32[]{:S(2)}) collective-permute-start(f32[32,18,1]{2,1,0:T(8,128)S(1)} %get-tuple-element.363), channel_id=1, source_target_pairs={{1,0},{2,1},{4,3},{5,4},{7,6},{8,7},{10,9},{11,10},{13,12},{14,13}... | collective-permute-start | bytes 6920 | tf_op jit(solution)/shard_map/while/body/eval_jaxpr/ppermute | solution.py:23
  (7 other events, 178.3 us)
Sparse Core Ops, SparseCore 0:
  11.2 99.6 all-gather.1
  410.6 209.5 reduce-scatter.1
where the time goes:
time: 633 us; the launch traced here: 627 us
  waiting for transfers between devices  413 us (65%)
  starting transfers between devices  178 us (28%)
  other arithmetic  17.1 us (3%)
  between operations  13.5 us (2%)
    reduce_scatter x1, waiting for transfers between devices, per_device(): increment = lax.psum_scatter(terms, 'mem', scatter_dimension=0, tiled=True)  210 us
    ppermute x34, starting transfers between devices, extended_2(): lax.ppermute(tail, axis, [(i, (i + 1) % count) for i in range(ends)])  134 us
    all_gather x1, waiting for transfers between devices, per_device(): all_planes = lax.all_gather(gradient, 'mem', axis=0, tiled=True)  84.2 us
    ppermute x34, waiting for transfers between devices, extended_2(): lax.ppermute(head, axis, [((i + 1) % count, i) for i in range(ends)])  63.2 us
    ppermute x34, waiting for transfers between devices, extended_2(): lax.ppermute(tail, axis, [(i, (i + 1) % count) for i in range(ends)])  55.2 us
    ppermute x34, starting transfers between devices, extended_2(): lax.ppermute(head, axis, [((i + 1) % count, i) for i in range(ends)])  44.1 us
  transfers between devices with their start and end apart: 70, of which 52 were waited for; matrix products, arithmetic and copies ran while one was open for 1% of the time, Pallas kernels for 0%

commit v1 on v0

v1 whole, which is shorter than its diff:
```python
import functools

import jax
import jax.numpy as jnp
from jax import lax
from jax.experimental import pallas as pl
from jax.experimental.pallas import tpu as pltpu
from jax.sharding import PartitionSpec as P

LEVELS = 32
STEPS = 8
TABLE = (0.03, 0.07, 0.12, 0.18)
MESH = pl.DeviceIdType.MESH

ZH = 4
YN = 8
BLOCKS = ZH * YN
LONG = YN // 2
SHORT = YN - 1 - LONG
F32 = jnp.float32


def ag_lengths(dz):
    return (LONG, SHORT) if dz % 2 == 0 else (SHORT, LONG)


def rs_lengths(dz):
    return (LONG, SHORT) if dz % 2 == 1 else (SHORT, LONG)


def kernel(
    gx_n, gy_n, offsets,
    grad_hbm, pert_hbm, classes_hbm, sea_hbm, out_ref,
    gall, pown, praw, psend, pother, codes, coef,
    wsend, wrecv, wown, field, back, back_other, s_own, s_other,
    rs_send, rs_recv, rz_send, rz_recv,
    loc, agz_s, agz_r, agy_s, agy_r, code_s, code_r, px_s, px_r, w_s, w_r,
    t_s, t_r, b_s, b_r, fw_s, fw_r, rsy_s, rsy_r, rsz_s, rsz_r,
):
    mem = lax.axis_index("mem")
    gx = lax.axis_index("gx")
    gy = lax.axis_index("gy")
    core = lax.rem(mem, 2)
    y = lax.rem(mem // 2, YN)
    zh = mem // (2 * YN)
    zdir = 1 - 2 * core

    def mem_at(z, yy):
        return {"mem": (lax.rem(z + 2 * ZH, ZH) * YN + lax.rem(yy + 2 * YN, YN)) * 2 + core}

    partner = {"mem": mem + zdir}
    y_up, y_down = mem_at(zh, y + 1), mem_at(zh, y - 1)
    z_fwd, z_bwd = mem_at(zh + zdir, y), mem_at(zh - zdir, y)
    y_next = (y_up, y_down)

    def z_of(dz):
        return (zh, zh - zdir, zh + zdir, zh + 2)[dz]

    def block(z, yy):
        return lax.rem(z + 2 * ZH, ZH) * YN + lax.rem(yy + 2 * YN, YN)

    def tile_of(dx, dy):
        return lax.rem(gx + dx + gx_n, gx_n), lax.rem(gy + dy + gy_n, gy_n)

    def remote(src, dst, ssem, rsem, where):
        return pltpu.make_async_remote_copy(
            src_ref=src, dst_ref=dst, send_sem=ssem, recv_sem=rsem,
            device_id=where, device_id_type=MESH,
        )

    def window(ref, tx, ty):
        return ref.at[
            :, pl.ds(pl.multiple_of(tx * 16, 16), 16), pl.ds(pl.multiple_of(ty * 128, 128), 128)
        ]

    barrier = pltpu.get_barrier_semaphore()
    tiles = [tile_of(dx, dy) for dx, dy in offsets]
    for where in (z_fwd, z_bwd, y_up, y_down, partner):
        pl.semaphore_signal(barrier, inc=1, device_id=where, device_id_type=MESH)
    for tx, ty in tiles:
        pl.semaphore_signal(barrier, inc=1, device_id={"gx": tx, "gy": ty}, device_id_type=MESH)
    mine = block(zh, y)
    c_grad = pltpu.make_async_copy(grad_hbm, gall.at[mine], loc.at[0])
    c_cls = pltpu.make_async_copy(classes_hbm, window(codes, gx, gy).at[pl.ds(0, 2)], loc.at[1])
    c_sea = pltpu.make_async_copy(sea_hbm, window(codes, gx, gy).at[pl.ds(2, 1)], loc.at[2])
    c_raw = pltpu.make_async_copy(pert_hbm.at[:, 1 - core], praw, loc.at[3])
    c_own = pltpu.make_async_copy(pert_hbm.at[:, core], pown, loc.at[4])
    for copy in (c_grad, c_cls, c_sea, c_raw, c_own):
        copy.start()
    c_grad.wait()
    pl.semaphore_wait(barrier, 5 + len(offsets))

    def ag_z(k):
        source = (z_of(0), z_of(0), z_of(1))[k]
        at = gall.at[block(source, y)]
        return remote(at, at, agz_s.at[k], agz_r.at[k], (z_fwd, z_bwd, z_fwd)[k])

    def ag_z_in(k):
        at = gall.at[block(z_of((1, 2, 3)[k]), y)]
        return remote(at, at, agz_s.at[k], agz_r.at[k], z_fwd)

    def ag_y(dz, way, hop):
        source = y - hop if way == 0 else y + hop
        at = gall.at[block(z_of(dz), source)]
        return remote(at, at, agy_s.at[dz, way, hop], agy_r.at[dz, way, hop], y_next[way])

    def ag_y_in(dz, way, hop):
        source = y - hop - 1 if way == 0 else y + hop + 1
        at = gall.at[block(z_of(dz), source)]
        return remote(at, at, agy_s.at[dz, way, hop], agy_r.at[dz, way, hop], y_next[way])

    ag_z(0).start()
    ag_z(1).start()
    ag_y(0, 0, 0).start()
    ag_y(0, 1, 0).start()

    c_cls.wait()
    c_sea.wait()
    for i, (tx, ty) in enumerate(tiles):
        at = window(codes, gx, gy)
        remote(at, at, code_s.at[i], code_r.at[i], {"gx": tx, "gy": ty}).start()
    c_raw.wait()

    @pl.loop(0, BLOCKS)
    def _(b):
        psend[b] = praw[b].astype(F32)

    remote(psend, pother, px_s, px_r, partner).start()
    c_own.wait()

    z_time = {0: 0.0, 1: 3.5, 2: 3.5, 3: 7.0}
    events = [(z_time[dz], 0, dz, 0, 0) for dz in (1, 2, 3)]
    for dz in range(ZH):
        for way in (0, 1):
            for hop in range(ag_lengths(dz)[way]):
                events.append((z_time[dz] + 2.0 * (hop + 1), 1, dz, way, hop))
    events.sort()
    late = len(events) - 6
    for number, (_, kind, dz, way, hop) in enumerate(events):
        if number == late:
            coefficients(gx_n, gy_n, offsets, tile_of, window, remote, codes, coef, code_s, code_r)
        if kind == 0:
            ag_z_in(dz - 1).wait_recv()
            if dz == 1:
                ag_z(2).start()
            ag_y(dz, 0, 0).start()
            ag_y(dz, 1, 0).start()
        else:
            ag_y_in(dz, way, hop).wait_recv()
            if hop + 1 < ag_lengths(dz)[way]:
                ag_y(dz, way, hop + 1).start()

    def weights(p_ref, w_ref):
        @pl.loop(0, 16, unroll=4)
        def _(e):
            one = lax.rem(11 * e, 16)
            two = lax.rem(11 * (e + 15), 16)

            def part(b, i):
                return p_ref[b, i].astype(F32) * gall[b, i]

            w_ref[lax.rem(2 * e + 3 * core, LEVELS)] = (
                part(one, 0) + part(one + 16, 0) + part(two, 2) + part(two + 16, 2)
            )
            w_ref[lax.rem(2 * e + 1 + 3 * core, LEVELS)] = part(one, 1) + part(one + 16, 1)

    swap_p = remote(psend, pother, px_s, px_r, partner)
    swap_p.wait_recv()
    weights(pother, wsend)
    swap_w = remote(wsend, wrecv, w_s, w_r, partner)
    swap_w.start()
    weights(pown, wown)
    swap_w.wait_recv()
    wown[...] = wown[...] + wrecv[...]

    def first_level(tx, ty):
        return 8 * tx + jnp.minimum(3 * ty, 5)

    for i, (tx, ty) in enumerate(tiles):
        remote(
            wown.at[pl.ds(first_level(tx, ty), 3)], window(field.at[0], gx, gy),
            t_s.at[i], t_r.at[i], {"gx": tx, "gy": ty},
        ).start()
    c_field = pltpu.make_async_copy(
        wown.at[pl.ds(first_level(gx, gy), 3)], window(field.at[0], gx, gy), loc.at[0]
    )
    c_field.start()
    c_field.wait()
    for i, (dx, dy) in enumerate(offsets):
        sx, sy = tile_of(-dx, -dy)
        remote(
            wown.at[pl.ds(first_level(gx, gy), 3)], window(field.at[0], sx, sy),
            t_s.at[i], t_r.at[i], {"gx": sx, "gy": sy},
        ).wait_recv()

    def stencil(source, target, base):
        for lev in range(3):
            v = field[source, lev]
            rows, cols = v.shape
            field[target, lev] = (
                coef[0] * v
                + coef[base] * pltpu.roll(v, rows - 1, 0)
                + coef[base + 1] * pltpu.roll(v, 1, 0)
                + coef[base + 2] * pltpu.roll(v, cols - 1, 1)
                + coef[base + 3] * pltpu.roll(v, 1, 1)
            )

    for base in (1, 5):
        @pl.loop(0, STEPS // 2)
        def _(_):
            stencil(0, 1, base)
            stencil(1, 0, base)

    def back_at(ref, tx, ty):
        return ref.at[tx, pl.ds(3 * ty, 3)]

    for i, (tx, ty) in enumerate(tiles):
        remote(
            window(field.at[0], tx, ty), back_at(back, gx, gy), b_s.at[i], b_r.at[i],
            {"gx": tx, "gy": ty},
        ).start()
    c_back = pltpu.make_async_copy(window(field.at[0], gx, gy), back_at(back, gx, gy), loc.at[0])
    c_back.start()
    c_back.wait()

    def forward(i, tx, ty):
        return remote(
            back_at(back, tx, ty), back_at(back_other, tx, ty), fw_s.at[i], fw_r.at[i], partner
        )

    forward(len(offsets), gx, gy).start()
    for i, (dx, dy) in enumerate(offsets):
        sx, sy = tile_of(-dx, -dy)
        remote(
            window(field.at[0], sx, sy), back_at(back, sx, sy), b_s.at[i], b_r.at[i],
            {"gx": sx, "gy": sy},
        ).wait_recv()
        forward(i, sx, sy).start()

    def gathered(ref, s_ref):
        levels = jnp.concatenate([ref[:, 0:6], ref[:, 7:9]], axis=1) * F32(1.0 / 63.0)
        levels = levels.reshape((LEVELS,) + levels.shape[2:])
        s_ref[pl.ds(0, LEVELS)] = levels
        s_ref[pl.ds(LEVELS, 2)] = levels[0:2]

    gathered(back, s_own)
    for i, (dx, dy) in enumerate(offsets):
        sx, sy = tile_of(-dx, -dy)
        forward(i, sx, sy).wait_recv()
    forward(len(offsets), gx, gy).wait_recv()
    gathered(back_other, s_other)

    def term(dz, yy):
        b = block(z_of(dz), yy)
        levels = pl.ds(lax.rem(6 * b + 3 * core, LEVELS), 3)
        return pown[b].astype(F32) * s_own[levels] + pother[b] * s_other[levels]

    def rs_y(dz, way, hop):
        return remote(
            rs_send.at[dz, way, hop], rs_recv.at[dz, way, hop],
            rsy_s.at[dz, way, hop], rsy_r.at[dz, way, hop], y_next[way],
        )

    def rs_z(k):
        return remote(
            rz_send.at[k], rz_recv.at[k], rsz_s.at[k], rsz_r.at[k], (z_fwd, z_fwd, z_bwd)[k]
        )

    order = (3, 2, 1, 0)
    for hop in range(LONG + 1):
        for dz in order:
            for way in (0, 1):
                left = rs_lengths(dz)[way] - hop
                if left > 0:
                    value = term(dz, y + left if way == 0 else y - left)
                    if hop > 0:
                        rs_y(dz, way, hop - 1).wait_recv()
                        value = value + rs_recv[dz, way, hop - 1]
                    rs_send[dz, way, hop] = value
                    rs_y(dz, way, hop).start()
            if hop == LONG:
                value = term(dz, y)
                for way in (0, 1):
                    last = rs_lengths(dz)[way] - 1
                    rs_y(dz, way, last).wait_recv()
                    value = value + rs_recv[dz, way, last]
                if dz == 3:
                    rz_send[0] = value
                    rs_z(0).start()
                elif dz == 2:
                    rs_z(0).wait_recv()
                    rz_send[1] = value + rz_recv[0]
                    rs_z(1).start()
                elif dz == 1:
                    rz_send[2] = value
                    rs_z(2).start()
                else:
                    rs_z(2).wait_recv()
                    value = value + rz_recv[2]
                    rs_z(1).wait_recv()
                    out_ref[...] = value + rz_recv[1]

    for k in range(3):
        ag_z(k).wait_send()
        rs_z(k).wait_send()
    for dz in range(ZH):
        for way in (0, 1):
            for hop in range(ag_lengths(dz)[way]):
                ag_y(dz, way, hop).wait_send()
            for hop in range(rs_lengths(dz)[way]):
                rs_y(dz, way, hop).wait_send()
    for i, (tx, ty) in enumerate(tiles):
        at = window(codes, gx, gy)
        where = {"gx": tx, "gy": ty}
        remote(at, at, code_s.at[i], code_r.at[i], where).wait_send()
        remote(
            wown.at[pl.ds(first_level(tx, ty), 3)], window(field.at[0], gx, gy),
            t_s.at[i], t_r.at[i], where,
        ).wait_send()
        remote(
            window(field.at[0], tx, ty), back_at(back, gx, gy), b_s.at[i], b_r.at[i], where
        ).wait_send()
    for i, (dx, dy) in enumerate(offsets):
        sx, sy = tile_of(-dx, -dy)
        forward(i, sx, sy).wait_send()
    forward(len(offsets), gx, gy).wait_send()
    swap_p.wait_send()
    swap_w.wait_send()


def coefficients(gx_n, gy_n, offsets, tile_of, window, remote, codes, coef, code_s, code_r):
    for i, (dx, dy) in enumerate(offsets):
        sx, sy = tile_of(-dx, -dy)
        at = window(codes, sx, sy)
        remote(at, at, code_s.at[i], code_r.at[i], {"gx": sx, "gy": sy}).wait_recv()

    def lookup(code):
        return sum(TABLE[c] * (code == c).astype(F32) for c in range(4))

    cx, cy = lookup(codes[0]), lookup(codes[1])
    mask = jnp.where(codes[2] == 1, F32(1.0), F32(0.3))
    rows, cols = cx.shape
    row = lax.broadcasted_iota(jnp.int32, cx.shape, 0)
    col = lax.broadcasted_iota(jnp.int32, cx.shape, 1)
    zero = jnp.zeros_like(cx)
    east = jnp.where(row < rows - 1, 0.5 * (cx + pltpu.roll(cx, rows - 1, 0)), zero)
    west = jnp.where(row > 0, 0.5 * (cx + pltpu.roll(cx, 1, 0)), zero)
    north = jnp.where(col < cols - 1, 0.5 * (cy + pltpu.roll(cy, cols - 1, 1)), zero)
    south = jnp.where(col > 0, 0.5 * (cy + pltpu.roll(cy, 1, 1)), zero)
    coef[0] = mask * (1.0 - (east + west + north + south))
    coef[1] = east * pltpu.roll(mask, rows - 1, 0)
    coef[2] = west * pltpu.roll(mask, 1, 0)
    coef[3] = north * pltpu.roll(mask, cols - 1, 1)
    coef[4] = south * pltpu.roll(mask, 1, 1)
    coef[5] = mask * east
    coef[6] = mask * west
    coef[7] = mask * north
    coef[8] = mask * south


def solution(mesh):
    gx_n, gy_n = mesh.shape["gx"], mesh.shape["gy"]
    offsets = [(dx, dy) for dx in range(gx_n) for dy in range(gy_n) if (dx, dy) != (0, 0)]
    others = len(offsets)

    def per_device(gradient, perturbation, classes, land_sea):
        tile = gradient.shape[1:]
        grid = (tile[0] * gx_n, tile[1] * gy_n)
        three = (3,) + tile
        dma = pltpu.SemaphoreType.DMA
        any_space = pl.BlockSpec(memory_space=pl.ANY)
        return pl.pallas_call(
            functools.partial(kernel, gx_n, gy_n, offsets),
            out_shape=jax.ShapeDtypeStruct(three, F32),
            in_specs=[any_space] * 4,
            out_specs=pl.BlockSpec(memory_space=pltpu.VMEM),
            scratch_shapes=[
                pltpu.VMEM((BLOCKS,) + three, F32),
                pltpu.VMEM((BLOCKS,) + three, jnp.bfloat16),
                pltpu.VMEM((BLOCKS,) + three, jnp.bfloat16),
                pltpu.VMEM((BLOCKS,) + three, F32),
                pltpu.VMEM((BLOCKS,) + three, F32),
                pltpu.VMEM((3,) + grid, jnp.int32),
                pltpu.VMEM((9,) + grid, F32),
                pltpu.VMEM((LEVELS,) + tile, F32),
                pltpu.VMEM((LEVELS,) + tile, F32),
                pltpu.VMEM((LEVELS,) + tile, F32),
                pltpu.VMEM((2, 3) + grid, F32),
                pltpu.VMEM((gx_n, 3 * gy_n) + tile, F32),
                pltpu.VMEM((gx_n, 3 * gy_n) + tile, F32),
                pltpu.VMEM((LEVELS + 2,) + tile, F32),
                pltpu.VMEM((LEVELS + 2,) + tile, F32),
                pltpu.VMEM((ZH, 2, LONG) + three, F32),
                pltpu.VMEM((ZH, 2, LONG) + three, F32),
                pltpu.VMEM((3,) + three, F32),
                pltpu.VMEM((3,) + three, F32),
                dma((5,)),
                dma((3,)), dma((3,)),
                dma((ZH, 2, LONG)), dma((ZH, 2, LONG)),
                dma((others,)), dma((others,)),
                dma, dma, dma, dma,
                dma((others,)), dma((others,)),
                dma((others,)), dma((others,)),
                dma((others + 1,)), dma((others + 1,)),
                dma((ZH, 2, LONG)), dma((ZH, 2, LONG)),
                dma((3,)), dma((3,)),
            ],
            compiler_params=pltpu.CompilerParams(collective_id=0, has_side_effects=True),
        )(
            gradient,
            perturbation.reshape((BLOCKS, 2) + three),
            classes,
            land_sea.reshape((1,) + tile),
        )

    placed = (P("mem", "gx", "gy"), P("mem", None, "gx", "gy"), P(None, "gx", "gy"), P("gx", "gy"))
    return jax.shard_map(
        per_device, mesh=mesh, in_specs=placed, out_specs=P("mem", "gx", "gy"), check_vma=False
    )
```

time: 633 us -> 84.8 us (0.13)
  the two profiles are of different devices: /device:TPU:1 before, /device:TPU:2 now
where the time goes in v1:
time: 84.8 us; the launch traced here: 84.6 us
  Pallas kernels  83.3 us (98%)
  local copies, waits for them, and re-layouts  1.35 us (2%)
    pallas_call x1, Pallas kernels, per_device(): pl.pallas_call(functools.partial(kernel, gx_n, gy_n, offsets), out_shape=...  83.3 us

profile of v1, /device:TPU:2, one launch (start us, length us, event | category | flops | bytes accessed | tf_op | source)
XLA Modules:
  0.0 84.6 jit_solution(778613928735958172)
XLA Ops:
  0.0 83.3 %shard_map.46 = f32[3,16,128]{2,1,0:T(8,128)} custom-call(f32[3,16,128]{2,1,0:T(8,128)} %grad_hbm.1, bf16[32,2,3,16,128]{4,3,2,1,0:T(8,128)(2,1)} %bitcast.2, s32[2,16,128]{2,1,0:T(8,128)} %classes_hbm.1, s32[1,16,128]{2,1,0:T(8,128)} %bitcast.3), custom_call_target="tpu_custom_call" | custom-call | tf_op jit(solution)/shard_map/pallas_call | solution.py:372
  83.3 1.3 %copy.6 = f32[3,16,128]{2,1,0:T(8,128)} copy(f32[3,16,128]{2,1,0:T(8,128)} %shard_map.46) | data formatting | bytes 49152

commit v2 on v1

v2 whole, which is shorter than its diff:
```python
import functools

import jax
import jax.numpy as jnp
from jax import lax
from jax.experimental import pallas as pl
from jax.experimental.pallas import tpu as pltpu
from jax.sharding import PartitionSpec as P

LEVELS = 32
STEPS = 8
TABLE = (0.03, 0.07, 0.12, 0.18)
MESH = pl.DeviceIdType.MESH

ZH = 4
YN = 8
BLOCKS = ZH * YN
F32 = jnp.float32

HOPS = (1, 2, -1, -2, 1, 2, -1)
SOURCES = (-1, -2, 1, 2, -3, -4, 3)


def kernel(
    gx_n, gy_n, offsets,
    grad_hbm, pert_hbm, classes_hbm, sea_hbm, out_ref,
    gall, pown, praw, psend, pother, codes, coef,
    wsend, wrecv, wown, field, back, back_other, s_own, s_other,
    rs_send, rs_recv, rz_send, rz_recv,
    loc, agz_s, agz_r, agy_s, agy_r, code_s, code_r, px_s, px_r, w_s, w_r,
    t_s, t_r, b_s, b_r, fw_s, fw_r, rsy_s, rsy_r, rsz_s, rsz_r,
):
    mem = lax.axis_index("mem")
    gx = lax.axis_index("gx")
    gy = lax.axis_index("gy")
    core = lax.rem(mem, 2)
    y = lax.rem(mem // 2, YN)
    zh = mem // (2 * YN)

    def mem_at(z, yy):
        return {"mem": block(z, yy) * 2 + core}

    partner = {"mem": mem + 1 - 2 * core}

    def z_of(dz):
        return zh + (0, 1, -1, 2)[dz]

    def way(dz):
        return 1 if dz % 2 == 0 else -1

    def block(z, yy):
        return lax.rem(z + ZH, ZH) * YN + lax.rem(yy + YN, YN)

    def tile_of(dx, dy):
        return lax.rem(gx + dx + gx_n, gx_n), lax.rem(gy + dy + gy_n, gy_n)

    sent = []

    def remote(src, dst, ssem, rsem, where):
        return pltpu.make_async_remote_copy(
            src_ref=src, dst_ref=dst, send_sem=ssem, recv_sem=rsem,
            device_id=where, device_id_type=MESH,
        )

    def send(copy):
        copy.start()
        sent.append(copy)

    def window(ref, tx, ty):
        return ref.at[
            :, pl.ds(pl.multiple_of(tx * 16, 16), 16), pl.ds(pl.multiple_of(ty * 128, 128), 128)
        ]

    barrier = pltpu.get_barrier_semaphore()
    tiles = [tile_of(dx, dy) for dx, dy in offsets]
    near = [mem_at(zh, y + d) for d in (1, -1, 2, -2)] + [mem_at(z_of(dz), y) for dz in (1, 2, 3)]
    near.append(partner)
    for where in near:
        pl.semaphore_signal(barrier, inc=1, device_id=where, device_id_type=MESH)
    for tx, ty in tiles:
        pl.semaphore_signal(barrier, inc=1, device_id={"gx": tx, "gy": ty}, device_id_type=MESH)
    mine = block(zh, y)
    c_grad = pltpu.make_async_copy(grad_hbm, gall.at[mine], loc.at[0])
    c_cls = pltpu.make_async_copy(classes_hbm, window(codes, gx, gy).at[pl.ds(0, 2)], loc.at[1])
    c_sea = pltpu.make_async_copy(sea_hbm, window(codes, gx, gy).at[pl.ds(2, 1)], loc.at[2])
    c_raw = pltpu.make_async_copy(pert_hbm.at[:, 1 - core], praw, loc.at[3])
    c_own = pltpu.make_async_copy(pert_hbm.at[:, core], pown, loc.at[4])
    for copy in (c_grad, c_cls, c_sea, c_raw, c_own):
        copy.start()
    c_grad.wait()
    pl.semaphore_wait(barrier, len(near) + len(offsets))

    def ag_z(dz):
        at = gall.at[mine]
        return remote(at, at, agz_s.at[dz], agz_r.at[dz], mem_at(z_of(dz), y))

    def ag_z_in(dz):
        k = (0, 2, 1, 3)[dz]
        at = gall.at[block(z_of(dz), y)]
        return remote(at, at, agz_s.at[k], agz_r.at[k], mem_at(z_of(dz), y))

    def ag_y(dz, m):
        hop = HOPS[m] * way(dz)
        at = gall.at[block(z_of(dz), y + SOURCES[m] * way(dz) + hop)]
        return remote(at, at, agy_s.at[dz, m], agy_r.at[dz, m], mem_at(zh, y + hop))

    def ag_y_in(dz, m):
        hop = HOPS[m] * way(dz)
        at = gall.at[block(z_of(dz), y + SOURCES[m] * way(dz))]
        return remote(at, at, agy_s.at[dz, m], agy_r.at[dz, m], mem_at(zh, y - hop))

    def ag_first(dz):
        for m in (1, 3, 0, 2):
            send(ag_y(dz, m))

    def ag_second(dz):
        ag_y_in(dz, 1).wait_recv()
        send(ag_y(dz, 5))
        send(ag_y(dz, 4))
        ag_y_in(dz, 3).wait_recv()
        send(ag_y(dz, 6))

    for dz in (3, 1, 2):
        send(ag_z(dz))
    ag_first(0)

    c_cls.wait()
    c_sea.wait()
    for i, (tx, ty) in enumerate(tiles):
        at = window(codes, gx, gy)
        send(remote(at, at, code_s.at[i], code_r.at[i], {"gx": tx, "gy": ty}))
    c_raw.wait()

    @pl.loop(0, BLOCKS)
    def _(b):
        psend[b] = praw[b].astype(F32)

    swap_p = remote(psend, pother, px_s, px_r, partner)
    send(swap_p)
    c_own.wait()

    wown[...] = jnp.zeros_like(wown)
    wsend[...] = jnp.zeros_like(wsend)

    def add_up(dz, p_ref, w_ref):
        @pl.loop(0, YN, unroll=2)
        def _(yy):
            b = block(z_of(dz), yy)
            levels = pl.ds(lax.rem(6 * b + 3 * core, LEVELS), 3)
            w_ref[levels] = w_ref[levels] + p_ref[b].astype(F32) * gall[b]

    def ag_rest(dz):
        for m in (0, 2, 4, 6, 5):
            ag_y_in(dz, m).wait_recv()

    def wrap(w_ref):
        w_ref[pl.ds(0, 2)] = w_ref[pl.ds(0, 2)] + w_ref[pl.ds(LEVELS, 2)]

    ag_second(0)
    for dz in (1, 2, 3):
        ag_z_in(dz).wait_recv()
        ag_first(dz)
    ag_second(1)
    ag_second(2)
    swap_p.wait_recv()
    ag_rest(0)
    add_up(0, pother, wsend)
    add_up(0, pown, wown)
    ag_second(3)
    coefficients(offsets, tile_of, window, remote, codes, coef, code_s, code_r)
    for dz in (1, 2):
        ag_rest(dz)
        add_up(dz, pother, wsend)
        add_up(dz, pown, wown)
    ag_rest(3)
    add_up(3, pother, wsend)
    wrap(wsend)
    swap_w = remote(wsend, wrecv, w_s, w_r, partner)
    send(swap_w)
    add_up(3, pown, wown)
    wrap(wown)
    swap_w.wait_recv()
    wown[...] = wown[...] + wrecv[...]

    def first_level(tx, ty):
        return 8 * tx + jnp.minimum(3 * ty, 5)

    for i, (tx, ty) in enumerate(tiles):
        send(remote(
            wown.at[pl.ds(first_level(tx, ty), 3)], window(field.at[0], gx, gy),
            t_s.at[i], t_r.at[i], {"gx": tx, "gy": ty},
        ))
    c_field = pltpu.make_async_copy(
        wown.at[pl.ds(first_level(gx, gy), 3)], window(field.at[0], gx, gy), loc.at[0]
    )
    c_field.start()
    c_field.wait()
    for i, (dx, dy) in enumerate(offsets):
        sx, sy = tile_of(-dx, -dy)
        remote(
            wown.at[pl.ds(first_level(gx, gy), 3)], window(field.at[0], sx, sy),
            t_s.at[i], t_r.at[i], {"gx": sx, "gy": sy},
        ).wait_recv()

    def stencil(source, target, base):
        for lev in range(3):
            v = field[source, lev]
            rows, cols = v.shape
            field[target, lev] = (
                coef[0] * v
                + coef[base] * pltpu.roll(v, rows - 1, 0)
                + coef[base + 1] * pltpu.roll(v, 1, 0)
                + coef[base + 2] * pltpu.roll(v, cols - 1, 1)
                + coef[base + 3] * pltpu.roll(v, 1, 1)
            )

    for base in (1, 5):
        @pl.loop(0, STEPS // 2)
        def _(_):
            stencil(0, 1, base)
            stencil(1, 0, base)

    def back_at(ref, tx, ty):
        return ref.at[tx, pl.ds(3 * ty, 3)]

    for i, (tx, ty) in enumerate(tiles):
        send(remote(
            window(field.at[0], tx, ty), back_at(back, gx, gy), b_s.at[i], b_r.at[i],
            {"gx": tx, "gy": ty},
        ))
    c_back = pltpu.make_async_copy(window(field.at[0], gx, gy), back_at(back, gx, gy), loc.at[0])
    c_back.start()
    c_back.wait()

    def forward(i, tx, ty):
        return remote(
            back_at(back, tx, ty), back_at(back_other, tx, ty), fw_s.at[i], fw_r.at[i], partner
        )

    send(forward(len(offsets), gx, gy))
    for i, (dx, dy) in enumerate(offsets):
        sx, sy = tile_of(-dx, -dy)
        remote(
            window(field.at[0], sx, sy), back_at(back, sx, sy), b_s.at[i], b_r.at[i],
            {"gx": sx, "gy": sy},
        ).wait_recv()
        send(forward(i, sx, sy))

    def gathered(ref, s_ref):
        levels = jnp.concatenate([ref[:, 0:6], ref[:, 7:9]], axis=1) * F32(1.0 / 63.0)
        levels = levels.reshape((LEVELS,) + levels.shape[2:])
        s_ref[pl.ds(0, LEVELS)] = levels
        s_ref[pl.ds(LEVELS, 2)] = levels[0:2]

    gathered(back, s_own)
    for i, (dx, dy) in enumerate(offsets):
        sx, sy = tile_of(-dx, -dy)
        forward(i, sx, sy).wait_recv()
    forward(len(offsets), gx, gy).wait_recv()
    gathered(back_other, s_other)

    def term(dz, yy):
        b = block(z_of(dz), yy)
        levels = pl.ds(lax.rem(6 * b + 3 * core, LEVELS), 3)
        return pown[b].astype(F32) * s_own[levels] + pother[b] * s_other[levels]

    def rs_y(dz, m):
        return remote(
            rs_send.at[dz, m], rs_recv.at[dz, m], rsy_s.at[dz, m], rsy_r.at[dz, m],
            mem_at(zh, y + HOPS[m] * way(dz)),
        )

    def rs_put(dz, m, distance, parts=()):
        value = term(dz, y + distance * way(dz))
        for part in parts:
            rs_y(dz, part).wait_recv()
            value = value + rs_recv[dz, part]
        rs_send[dz, m] = value
        send(rs_y(dz, m))

    def rs_z(dz):
        return remote(
            rz_send.at[dz], rz_recv.at[dz], rsz_s.at[dz], rsz_r.at[dz], mem_at(z_of(dz), y)
        )

    order = (3, 1, 2, 0)
    for dz in order:
        rs_put(dz, 5, 4)
        rs_put(dz, 4, 3)
        rs_put(dz, 6, -3)
    for dz in order:
        rs_put(dz, 0, 1)
        rs_put(dz, 2, -1)
        rs_put(dz, 1, 2, (4, 5))
        rs_put(dz, 3, -2, (6,))
    for dz in order:
        value = term(dz, y)
        for m in (0, 2, 1, 3):
            rs_y(dz, m).wait_recv()
            value = value + rs_recv[dz, m]
        if dz == 0:
            for k in (1, 2, 3):
                rs_z(k).wait_recv()
                value = value + rz_recv[k]
            out_ref[...] = value
        else:
            rz_send[dz] = value
            send(rs_z(dz))

    for copy in sent:
        copy.wait_send()


def coefficients(offsets, tile_of, window, remote, codes, coef, code_s, code_r):
    for i, (dx, dy) in enumerate(offsets):
        sx, sy = tile_of(-dx, -dy)
        at = window(codes, sx, sy)
        remote(at, at, code_s.at[i], code_r.at[i], {"gx": sx, "gy": sy}).wait_recv()

    def lookup(code):
        return sum(TABLE[c] * (code == c).astype(F32) for c in range(4))

    cx, cy = lookup(codes[0]), lookup(codes[1])
    mask = jnp.where(codes[2] == 1, F32(1.0), F32(0.3))
    rows, cols = cx.shape
    row = lax.broadcasted_iota(jnp.int32, cx.shape, 0)
    col = lax.broadcasted_iota(jnp.int32, cx.shape, 1)
    zero = jnp.zeros_like(cx)
    east = jnp.where(row < rows - 1, 0.5 * (cx + pltpu.roll(cx, rows - 1, 0)), zero)
    west = jnp.where(row > 0, 0.5 * (cx + pltpu.roll(cx, 1, 0)), zero)
    north = jnp.where(col < cols - 1, 0.5 * (cy + pltpu.roll(cy, cols - 1, 1)), zero)
    south = jnp.where(col > 0, 0.5 * (cy + pltpu.roll(cy, 1, 1)), zero)
    coef[0] = mask * (1.0 - (east + west + north + south))
    coef[1] = east * pltpu.roll(mask, rows - 1, 0)
    coef[2] = west * pltpu.roll(mask, 1, 0)
    coef[3] = north * pltpu.roll(mask, cols - 1, 1)
    coef[4] = south * pltpu.roll(mask, 1, 1)
    coef[5] = mask * east
    coef[6] = mask * west
    coef[7] = mask * north
    coef[8] = mask * south


def solution(mesh):
    gx_n, gy_n = mesh.shape["gx"], mesh.shape["gy"]
    offsets = [(dx, dy) for dx in range(gx_n) for dy in range(gy_n) if (dx, dy) != (0, 0)]
    others = len(offsets)

    def per_device(gradient, perturbation, classes, land_sea):
        tile = gradient.shape[1:]
        grid = (tile[0] * gx_n, tile[1] * gy_n)
        three = (3,) + tile
        dma = pltpu.SemaphoreType.DMA
        any_space = pl.BlockSpec(memory_space=pl.ANY)
        return pl.pallas_call(
            functools.partial(kernel, gx_n, gy_n, offsets),
            out_shape=jax.ShapeDtypeStruct(three, F32),
            in_specs=[any_space] * 4,
            out_specs=pl.BlockSpec(memory_space=pltpu.VMEM),
            scratch_shapes=[
                pltpu.VMEM((BLOCKS,) + three, F32),
                pltpu.VMEM((BLOCKS,) + three, jnp.bfloat16),
                pltpu.VMEM((BLOCKS,) + three, jnp.bfloat16),
                pltpu.VMEM((BLOCKS,) + three, F32),
                pltpu.VMEM((BLOCKS,) + three, F32),
                pltpu.VMEM((3,) + grid, jnp.int32),
                pltpu.VMEM((9,) + grid, F32),
                pltpu.VMEM((LEVELS + 2,) + tile, F32),
                pltpu.VMEM((LEVELS + 2,) + tile, F32),
                pltpu.VMEM((LEVELS + 2,) + tile, F32),
                pltpu.VMEM((2, 3) + grid, F32),
                pltpu.VMEM((gx_n, 3 * gy_n) + tile, F32),
                pltpu.VMEM((gx_n, 3 * gy_n) + tile, F32),
                pltpu.VMEM((LEVELS + 2,) + tile, F32),
                pltpu.VMEM((LEVELS + 2,) + tile, F32),
                pltpu.VMEM((ZH, 7) + three, F32),
                pltpu.VMEM((ZH, 7) + three, F32),
                pltpu.VMEM((ZH,) + three, F32),
                pltpu.VMEM((ZH,) + three, F32),
                dma((5,)),
                dma((ZH,)), dma((ZH,)),
                dma((ZH, 7)), dma((ZH, 7)),
                dma((others,)), dma((others,)),
                dma, dma, dma, dma,
                dma((others,)), dma((others,)),
                dma((others,)), dma((others,)),
                dma((others + 1,)), dma((others + 1,)),
                dma((ZH, 7)), dma((ZH, 7)),
                dma((ZH,)), dma((ZH,)),
            ],
            compiler_params=pltpu.CompilerParams(collective_id=0, has_side_effects=True),
        )(
            gradient,
            perturbation.reshape((BLOCKS, 2) + three),
            classes,
            land_sea.reshape((1,) + tile),
        )

    placed = (P("mem", "gx", "gy"), P("mem", None, "gx", "gy"), P(None, "gx", "gy"), P("gx", "gy"))
    return jax.shard_map(
        per_device, mesh=mesh, in_specs=placed, out_specs=P("mem", "gx", "gy"), check_vma=False
    )
```

time: 84.8 us -> 75.4 us (0.89)
  the two profiles are of different devices: /device:TPU:2 before, /device:TPU:1 now
where the time goes in v2:
time: 75.4 us; the launch traced here: 75.2 us
  Pallas kernels  73.8 us (98%)
  local copies, waits for them, and re-layouts  1.35 us (2%)
    pallas_call x1, Pallas kernels, per_device(): pl.pallas_call(functools.partial(kernel, gx_n, gy_n, offsets), out_shape=...  73.8 us

profile of v2, /device:TPU:1, one launch (start us, length us, event | category | flops | bytes accessed | tf_op | source)
XLA Modules:
  0.0 75.2 jit_solution(2546589289592522077)
XLA Ops:
  0.0 73.8 %shard_map.46 = f32[3,16,128]{2,1,0:T(8,128)} custom-call(f32[3,16,128]{2,1,0:T(8,128)} %grad_hbm.1, bf16[32,2,3,16,128]{4,3,2,1,0:T(8,128)(2,1)} %bitcast.2, s32[2,16,128]{2,1,0:T(8,128)} %classes_hbm.1, s32[1,16,128]{2,1,0:T(8,128)} %bitcast.3), custom_call_target="tpu_custom_call" | custom-call | tf_op jit(solution)/shard_map/pallas_call | solution.py:355
  73.8 1.3 %copy.6 = f32[3,16,128]{2,1,0:T(8,128)} copy(f32[3,16,128]{2,1,0:T(8,128)} %shard_map.46) | data formatting | bytes 49152

commit v3 on v2

--- a/solution.py
+++ b/solution.py
@@ -343,7 +343,8 @@
 
 def solution(mesh):
     gx_n, gy_n = mesh.shape["gx"], mesh.shape["gy"]
-    offsets = [(dx, dy) for dx in range(gx_n) for dy in range(gy_n) if (dx, dy) != (0, 0)]
+    offsets = [(dx, dy) for dx in (2, 1, 3, 0) for dy in range(1, gy_n)]
+    offsets += [(dx, 0) for dx in (2, 1, 3)]
     others = len(offsets)
 
     def per_device(gradient, perturbation, classes, land_sea):

time: 75.4 us -> 73.7 us (0.977)
  Pallas kernels: 73.8 us -> 71.8 us
    pallas_call x1, Pallas kernels: 73.8 us -> 71.8 us  [per_device(): pl.pallas_call(functools.partial(kernel, gx_n, gy_n, offsets), out_shape=...]
where the time goes in v3:
time: 73.7 us; the launch traced here: 73.2 us
  Pallas kernels  71.8 us (97%)
  local copies, waits for them, and re-layouts  1.35 us (2%)
    pallas_call x1, Pallas kernels, per_device(): pl.pallas_call(functools.partial(kernel, gx_n, gy_n, offsets), out_shape=...  71.8 us

profile of v3, /device:TPU:1, one launch (start us, length us, event | category | flops | bytes accessed | tf_op | source)
XLA Modules:
  0.0 73.2 jit_solution(18063646648022186802)
XLA Ops:
  0.0 71.8 %shard_map.46 = f32[3,16,128]{2,1,0:T(8,128)} custom-call(f32[3,16,128]{2,1,0:T(8,128)} %grad_hbm.1, bf16[32,2,3,16,128]{4,3,2,1,0:T(8,128)(2,1)} %bitcast.2, s32[2,16,128]{2,1,0:T(8,128)} %classes_hbm.1, s32[1,16,128]{2,1,0:T(8,128)} %bitcast.3), custom_call_target="tpu_custom_call" | custom-call | tf_op jit(solution)/shard_map/pallas_call | solution.py:356
  71.9 1.3 %copy.6 = f32[3,16,128]{2,1,0:T(8,128)} copy(f32[3,16,128]{2,1,0:T(8,128)} %shard_map.46) | data formatting | bytes 49152

commit v4 on v3

--- a/solution.py
+++ b/solution.py
@@ -17,6 +17,7 @@
 BLOCKS = ZH * YN
 F32 = jnp.float32
 
+GROUPS = ((0, 1), (1, 2))
 HOPS = (1, 2, -1, -2, 1, 2, -1)
 SOURCES = (-1, -2, 1, 2, -3, -4, 3)
 
@@ -185,66 +186,71 @@
     def first_level(tx, ty):
         return 8 * tx + jnp.minimum(3 * ty, 5)
 
-    for i, (tx, ty) in enumerate(tiles):
-        send(remote(
-            wown.at[pl.ds(first_level(tx, ty), 3)], window(field.at[0], gx, gy),
-            t_s.at[i], t_r.at[i], {"gx": tx, "gy": ty},
-        ))
+    def level_out(g, i, tx, ty):
+        at, n = GROUPS[g]
+        return remote(
+            wown.at[pl.ds(first_level(tx, ty) + at, n)],
+            window(field.at[0], gx, gy).at[pl.ds(at, n)],
+            t_s.at[g, i], t_r.at[g, i], {"gx": tx, "gy": ty},
+        )
+
+    def level_back(g, i, tx, ty):
+        at, n = GROUPS[g]
+        return remote(
+            window(field.at[0], tx, ty).at[pl.ds(at, n)],
+            back.at[gx, pl.ds(3 * gy + at, n)],
+            b_s.at[g, i], b_r.at[g, i], {"gx": tx, "gy": ty},
+        )
+
+    def forward(i, tx, ty):
+        at = pl.ds(3 * ty, 3)
+        return remote(back.at[tx, at], back_other.at[tx, at], fw_s.at[i], fw_r.at[i], partner)
+
     c_field = pltpu.make_async_copy(
         wown.at[pl.ds(first_level(gx, gy), 3)], window(field.at[0], gx, gy), loc.at[0]
     )
     c_field.start()
+    for g in range(len(GROUPS)):
+        for i, (tx, ty) in enumerate(tiles):
+            send(level_out(g, i, tx, ty))
     c_field.wait()
-    for i, (dx, dy) in enumerate(offsets):
-        sx, sy = tile_of(-dx, -dy)
-        remote(
-            wown.at[pl.ds(first_level(gx, gy), 3)], window(field.at[0], sx, sy),
-            t_s.at[i], t_r.at[i], {"gx": sx, "gy": sy},
-        ).wait_recv()
-
-    def stencil(source, target, base):
-        for lev in range(3):
-            v = field[source, lev]
-            rows, cols = v.shape
-            field[target, lev] = (
-                coef[0] * v
-                + coef[base] * pltpu.roll(v, rows - 1, 0)
-                + coef[base + 1] * pltpu.roll(v, 1, 0)
-                + coef[base + 2] * pltpu.roll(v, cols - 1, 1)
-                + coef[base + 3] * pltpu.roll(v, 1, 1)
-            )
-
-    for base in (1, 5):
-        @pl.loop(0, STEPS // 2)
-        def _(_):
-            stencil(0, 1, base)
-            stencil(1, 0, base)
-
-    def back_at(ref, tx, ty):
-        return ref.at[tx, pl.ds(3 * ty, 3)]
-
-    for i, (tx, ty) in enumerate(tiles):
-        send(remote(
-            window(field.at[0], tx, ty), back_at(back, gx, gy), b_s.at[i], b_r.at[i],
-            {"gx": tx, "gy": ty},
-        ))
-    c_back = pltpu.make_async_copy(window(field.at[0], gx, gy), back_at(back, gx, gy), loc.at[0])
+    sources = [tile_of(-dx, -dy) for dx, dy in offsets]
+
+    def step(v, base):
+        rows, cols = v.shape
+        return (
+            coef[0] * v
+            + coef[base] * pltpu.roll(v, rows - 1, 0)
+            + coef[base + 1] * pltpu.roll(v, 1, 0)
+            + coef[base + 2] * pltpu.roll(v, cols - 1, 1)
+            + coef[base + 3] * pltpu.roll(v, 1, 1)
+        )
+
+    for g in range(len(GROUPS)):
+        for i in range(len(offsets)):
+            level_out(g, i, gx, gy).wait_recv()
+        at, n = GROUPS[g]
+        for base in (1, 5):
+            @pl.loop(0, STEPS // 2)
+            def _(_):
+                for lev in range(at, at + n):
+                    field[1, lev] = step(field[0, lev], base)
+                for lev in range(at, at + n):
+                    field[0, lev] = step(field[1, lev], base)
+        for i, (tx, ty) in enumerate(tiles):
+            send(level_back(g, i, tx, ty))
+    c_back = pltpu.make_async_copy(
+        window(field.at[0], gx, gy), back.at[gx, pl.ds(3 * gy, 3)], loc.at[0],
+    )
     c_back.start()
     c_back.wait()
-
-    def forward(i, tx, ty):
-        return remote(
-            back_at(back, tx, ty), back_at(back_other, tx, ty), fw_s.at[i], fw_r.at[i], partner
-        )
-
     send(forward(len(offsets), gx, gy))
-    for i, (dx, dy) in enumerate(offsets):
-        sx, sy = tile_of(-dx, -dy)
-        remote(
-            window(field.at[0], sx, sy), back_at(back, sx, sy), b_s.at[i], b_r.at[i],
-            {"gx": sx, "gy": sy},
-        ).wait_recv()
-        send(forward(i, sx, sy))
+    last = len(GROUPS) - 1
+    for g in range(len(GROUPS)):
+        for i, (sx, sy) in enumerate(sources):
+            level_back(g, i, sx, sy).wait_recv()
+            if g == last:
+                send(forward(i, sx, sy))
 
     def gathered(ref, s_ref):
         levels = jnp.concatenate([ref[:, 0:6], ref[:, 7:9]], axis=1) * F32(1.0 / 63.0)
@@ -253,10 +259,8 @@
         s_ref[pl.ds(LEVELS, 2)] = levels[0:2]
 
     gathered(back, s_own)
-    for i, (dx, dy) in enumerate(offsets):
-        sx, sy = tile_of(-dx, -dy)
+    for i, (sx, sy) in enumerate(sources + [(gx, gy)]):
         forward(i, sx, sy).wait_recv()
-    forward(len(offsets), gx, gy).wait_recv()
     gathered(back_other, s_other)
 
     def term(dz, yy):
@@ -383,8 +387,8 @@
                 dma((ZH, 7)), dma((ZH, 7)),
                 dma((others,)), dma((others,)),
                 dma, dma, dma, dma,
-                dma((others,)), dma((others,)),
-                dma((others,)), dma((others,)),
+                dma((2, others)), dma((2, others)),
+                dma((2, others)), dma((2, others)),
                 dma((others + 1,)), dma((others + 1,)),
                 dma((ZH, 7)), dma((ZH, 7)),
                 dma((ZH,)), dma((ZH,)),

time: 73.7 us -> 72.4 us (0.982)
  Pallas kernels: 71.8 us -> 70.3 us
    pallas_call x1, Pallas kernels: 71.8 us -> 70.3 us  [per_device(): pl.pallas_call(functools.partial(kernel, gx_n, gy_n, offsets), out_shape=...]
where the time goes in v4:
time: 72.4 us; the launch traced here: 71.7 us
  Pallas kernels  70.3 us (97%)
  local copies, waits for them, and re-layouts  1.35 us (2%)
    pallas_call x1, Pallas kernels, per_device(): pl.pallas_call(functools.partial(kernel, gx_n, gy_n, offsets), out_shape=...  70.3 us

profile of v4, /device:TPU:1, one launch (start us, length us, event | category | flops | bytes accessed | tf_op | source)
XLA Modules:
  0.0 71.7 jit_solution(9529896072302513124)
XLA Ops:
  0.0 70.3 %shard_map.46 = f32[3,16,128]{2,1,0:T(8,128)} custom-call(f32[3,16,128]{2,1,0:T(8,128)} %grad_hbm.1, bf16[32,2,3,16,128]{4,3,2,1,0:T(8,128)(2,1)} %bitcast.2, s32[2,16,128]{2,1,0:T(8,128)} %classes_hbm.1, s32[1,16,128]{2,1,0:T(8,128)} %bitcast.3), custom_call_target="tpu_custom_call" | custom-call | tf_op jit(solution)/shard_map/pallas_call | solution.py:360
  70.3 1.3 %copy.6 = f32[3,16,128]{2,1,0:T(8,128)} copy(f32[3,16,128]{2,1,0:T(8,128)} %shard_map.46) | data formatting | bytes 49152

commit v5 on v4

--- a/solution.py
+++ b/solution.py
@@ -74,7 +74,7 @@
 
     barrier = pltpu.get_barrier_semaphore()
     tiles = [tile_of(dx, dy) for dx, dy in offsets]
-    near = [mem_at(zh, y + d) for d in (1, -1, 2, -2)] + [mem_at(z_of(dz), y) for dz in (1, 2, 3)]
+    near = [mem_at(z_of(dz), y) for dz in (3, 1, 2)] + [mem_at(zh, y + d) for d in (2, -2, 1, -1)]
     near.append(partner)
     for where in near:
         pl.semaphore_signal(barrier, inc=1, device_id=where, device_id_type=MESH)
@@ -345,6 +345,10 @@
     coef[8] = mask * south
 
 
+def hand_on(source, target):
+    target[...] = source[...]
+
+
 def solution(mesh):
     gx_n, gy_n = mesh.shape["gx"], mesh.shape["gy"]
     offsets = [(dx, dy) for dx in (2, 1, 3, 0) for dy in range(1, gy_n)]
@@ -357,7 +361,7 @@
         three = (3,) + tile
         dma = pltpu.SemaphoreType.DMA
         any_space = pl.BlockSpec(memory_space=pl.ANY)
-        return pl.pallas_call(
+        increment = pl.pallas_call(
             functools.partial(kernel, gx_n, gy_n, offsets),
             out_shape=jax.ShapeDtypeStruct(three, F32),
             in_specs=[any_space] * 4,
@@ -400,6 +404,7 @@
             classes,
             land_sea.reshape((1,) + tile),
         )
+        return pl.pallas_call(hand_on, out_shape=jax.ShapeDtypeStruct(three, F32))(increment)
 
     placed = (P("mem", "gx", "gy"), P("mem", None, "gx", "gy"), P(None, "gx", "gy"), P("gx", "gy"))
     return jax.shard_map(

time: 72.4 us -> 72.2 us (level)
  local copies, waits for them, and re-layouts: 1.35 us -> 0 us
  Pallas kernels: 70.3 us -> 71.2 us
    pallas_call x0 -> x1, Pallas kernels: none -> 1.35 us  [per_device(): pl.pallas_call(hand_on, out_shape=jax.ShapeDtypeStruct(three, F32))]
    unnamed x1 -> x0, local copies, waits for them, and re-layouts: 1.35 us -> none
where the time goes in v5:
time: 72.2 us; the launch traced here: 71.2 us
  Pallas kernels  71.2 us (99%)
    pallas_call x1, Pallas kernels, per_device(): pl.pallas_call(functools.partial(kernel, gx_n, gy_n, offsets), out_shape=...  69.8 us

profile of v5, /device:TPU:1, one launch (start us, length us, event | category | flops | bytes accessed | tf_op | source)
XLA Modules:
  0.0 71.2 jit_solution(14140134993620188115)
XLA Ops:
  0.0 69.8 %shard_map.46.source = f32[3,16,128]{2,1,0:T(8,128)} custom-call(f32[3,16,128]{2,1,0:T(8,128)} %grad_hbm.1, bf16[32,2,3,16,128]{4,3,2,1,0:T(8,128)(2,1)} %bitcast.2, s32[2,16,128]{2,1,0:T(8,128)} %classes_hbm.1, s32[1,16,128]{2,1,0:T(8,128)} %bitcast.3), custom_call_target="tpu_custom_call" | custom-call | tf_op jit(solution)/shard_map/pallas_call | solution.py:364
  69.9 1.3 %shard_map.47 = f32[3,16,128]{2,1,0:T(8,128)} custom-call(f32[3,16,128]{2,1,0:T(8,128)} %shard_map.46.source), custom_call_target="tpu_custom_call" | custom-call | tf_op jit(solution)/shard_map/pallas_call | solution.py:407

commit v6 on v5

--- a/solution.py
+++ b/solution.py
@@ -295,8 +295,8 @@
     for dz in order:
         rs_put(dz, 0, 1)
         rs_put(dz, 2, -1)
+        rs_put(dz, 3, -2, (6,))
         rs_put(dz, 1, 2, (4, 5))
-        rs_put(dz, 3, -2, (6,))
     for dz in order:
         value = term(dz, y)
         for m in (0, 2, 1, 3):

time: 72.2 us -> 72.4 us (level); the launches traced: 71.2 us -> 72.2 us
  Pallas kernels: 71.2 us -> 72.2 us
    pallas_call x1, Pallas kernels: 69.8 us -> 70.8 us  [per_device(): pl.pallas_call(functools.partial(kernel, gx_n, gy_n, offsets), out_shape=...]
where the time goes in v6:
time: 72.4 us; the launch traced here: 72.2 us
  Pallas kernels  72.2 us (100%)
    pallas_call x1, Pallas kernels, per_device(): pl.pallas_call(functools.partial(kernel, gx_n, gy_n, offsets), out_shape=...  70.8 us

profile of v6, /device:TPU:1, one launch (start us, length us, event | category | flops | bytes accessed | tf_op | source)
XLA Modules:
  0.0 72.2 jit_solution(1696103530612761286)
XLA Ops:
  0.0 70.8 %shard_map.46.source = f32[3,16,128]{2,1,0:T(8,128)} custom-call(f32[3,16,128]{2,1,0:T(8,128)} %grad_hbm.1, bf16[32,2,3,16,128]{4,3,2,1,0:T(8,128)(2,1)} %bitcast.2, s32[2,16,128]{2,1,0:T(8,128)} %classes_hbm.1, s32[1,16,128]{2,1,0:T(8,128)} %bitcast.3), custom_call_target="tpu_custom_call" | custom-call | tf_op jit(solution)/shard_map/pallas_call | solution.py:364
  70.8 1.3 %shard_map.47 = f32[3,16,128]{2,1,0:T(8,128)} custom-call(f32[3,16,128]{2,1,0:T(8,128)} %shard_map.46.source), custom_call_target="tpu_custom_call" | custom-call | tf_op jit(solution)/shard_map/pallas_call | solution.py:407
